TPU v7x, 512 devices: a whole 4x8x8 slice. The times are simulated.
512 devices in a mesh: space: 64 (over y, z_hi, core), bead: 8 (over x, z_lo).
Axes of the slice: x: 4, y: 8, z: 8 (z_hi: 4, z_lo: 2; z = z_hi * 2 + z_lo), core: 2. Of those that a mesh axis runs over, the one named last changes fastest.
Arguments:
- positions: float32 [32, 3, 8192], P('bead', None, 'space'), may hold values from 0 to 2
- momenta: float32 [32, 3, 8192], P('bead', None, 'space'), may hold values from -6 to 6
- masses: float32 [8192], P('space'), may hold values from 1 to 4
- features: bfloat16 [32, 8192, 128], P('bead', 'space'), may hold values from -6 to 6
- neighbours: int32 [64, 8192], P(None, 'space'), may hold values from 0 to 383
- images: int32 [64, 8192], P(None, 'space'), may hold values from 0 to 26
- face_map: int32 [2, 64, 128], P(None, 'space'), may hold values from 0 to 127, each once within a row
- w_query: bfloat16 [128, 128], replicated, may hold values from -0.5 to 0.5
- w_key: bfloat16 [128, 128], replicated, may hold values from -0.375 to 0.375
- w_value: bfloat16 [128, 128], replicated, may hold values from -2 to 2
- w_probe: bfloat16 [128, 128], replicated, may hold values from -0.5 to 0.5
- radial_rate: float32 [8], replicated, may hold values from 0.02 to 0.5
Outputs:
- new_positions: float32 [32, 3, 8192], P('bead', None, 'space')
- new_momenta: float32 [32, 3, 8192], P('bead', None, 'space')
Inputs may be any that keep to these rules, and one draw needn't show every extreme that they name: `neighbours`: each entry is a row of the atom's slab's extended table: own atoms first, then the ghosts from the lower slab, then those from the upper slab. `face_map`: each row of a slab's block lists every atom of that slab once.
All inputs are finite; a program needn't handle non-finite values.
Results may differ from a plain program's by a relative error of at most 0.0025.
Values may be sent and summed in bfloat16 or wider, within the bound.
No kernel may reach another device: no remote copies, remote signals or barrier semaphores. Data moves between devices by JAX's collectives and lax.ppermute only.
A program may use at most 64 MiB of HBM per device.

v0:
```python
import jax
import jax.numpy as jnp
from jax import lax
from jax.sharding import PartitionSpec as P

STIFFNESS = 1.3
BOX_LENGTH = 2.0
SCORE_CAP = 30.0


def padded(block, sides, width):
    for axis, dim in sides:
        count = lax.axis_size(axis)
        forward = [(i, i + 1) for i in range(count - 1)]
        forward.append((count - 1, 0))
        backward = [(target, source) for source, target in forward]
        low = lax.ppermute(
            lax.slice_in_dim(block, block.shape[dim] - width, None, axis=dim), axis, forward
        )
        high = lax.ppermute(lax.slice_in_dim(block, 0, width, axis=dim), axis, backward)
        block = jnp.concatenate([low, block, high], axis=dim)
    return block


def from_everyone(x, axis):
    length = lax.axis_size(axis)
    return lax.all_to_all(jnp.broadcast_to(x[None], (length, *x.shape)), axis, 0, 0, tiled=True)


def in_order(pieces, dim):
    lengths = list(pieces.shape[1:])
    lengths[dim] *= pieces.shape[0]
    return jnp.moveaxis(pieces, 0, dim).reshape(lengths)


def gathered_copies(x, axis, dim):
    pieces = from_everyone(x, axis)
    return in_order(pieces, dim)


def mode_table(bead_count):
    bead_column = jnp.arange(bead_count).astype(jnp.float32)[:, None]
    mode_row = jnp.arange(bead_count).astype(jnp.float32)[None, :]
    mode_index = jnp.arange(bead_count)[None, :] + jnp.zeros((bead_count, 1), jnp.int32)
    angles = 2.0 * jnp.pi * bead_column * mode_row / bead_count
    wave_norm = jnp.sqrt(jnp.float32(2.0 / bead_count))
    flat_norm = jnp.sqrt(jnp.float32(1.0 / bead_count))
    half_count = bead_count // 2
    entries = jnp.where(
        mode_index < half_count, wave_norm * jnp.cos(angles), wave_norm * jnp.sin(angles)
    )
    entries = jnp.where(mode_index == half_count, flat_norm * jnp.cos(angles), entries)
    entries = jnp.where(mode_index == 0, flat_norm + 0.0 * angles, entries)
    return entries


def frequencies(bead_count):
    mode_float = jnp.arange(bead_count).astype(jnp.float32)
    return 2.0 * STIFFNESS * jnp.sin(jnp.pi * mode_float / bead_count)


def propagate(mode_pos, mode_mom, masses, frequency):
    phase_turn = frequency[:, None, None]
    cosine_turn = jnp.cos(phase_turn)
    sine_turn = jnp.sin(phase_turn)
    safe_turn = jnp.where(phase_turn > 0, phase_turn, 1.0)
    drift_gain = jnp.where(phase_turn > 0, sine_turn / safe_turn, 1.0)
    mass_row = masses[None, None, :]
    next_pos = cosine_turn * mode_pos + drift_gain * mode_mom / mass_row
    next_mom = cosine_turn * mode_mom - mass_row * phase_turn * sine_turn * mode_pos
    return (next_pos, next_mom)


def image_offsets(images):
    offset_x = images % 3 - 1
    offset_y = images // 3 % 3 - 1
    offset_z = images // 9 - 1
    return BOX_LENGTH * jnp.stack([offset_x, offset_y, offset_z]).astype(jnp.float32)


def probe_matrices(own_features, w_query, w_key, w_value, w_probe, head_count):
    atom_count, channels = own_features.shape
    head_size = channels // head_count
    queries = jnp.dot(own_features, w_query, preferred_element_type=jnp.float32).reshape(
        atom_count, head_count, head_size
    )
    probes = jnp.dot(own_features, w_probe, preferred_element_type=jnp.float32).reshape(
        atom_count, head_count, head_size
    )
    key_heads = w_key.astype(jnp.float32).reshape(channels, head_count, head_size)
    value_heads = w_value.astype(jnp.float32).reshape(channels, head_count, head_size)
    key_probe = jnp.einsum("ahd,chd->ahc", queries, key_heads, precision=lax.Precision.HIGHEST)
    value_probe = jnp.einsum("ahd,chd->ahc", probes, value_heads, precision=lax.Precision.HIGHEST)
    return jnp.concatenate([key_probe, value_probe], axis=1).astype(jnp.bfloat16)


def attend_forces(pair_terms, offsets, radial_rate, head_size):
    head_count = radial_rate.shape[0]
    scores = pair_terms[:head_count] * head_size ** (-0.5)
    capped = SCORE_CAP * jnp.tanh(scores / SCORE_CAP)
    distance = jnp.sum(offsets * offsets, axis=0)
    logits = capped - radial_rate[:, None, None] * distance[None]
    weights = jnp.exp(logits)
    attention = weights / jnp.sum(weights, axis=1, keepdims=True)
    coupling = jnp.sum(attention * pair_terms[head_count:], axis=0) * (
        1.0 / (head_count * head_size**0.5)
    )
    return jnp.sum(coupling[None] * offsets, axis=1)


def split_pieces(coordinate_table):
    high_part = coordinate_table.astype(jnp.bfloat16)
    first_rest = coordinate_table - high_part.astype(jnp.float32)
    middle_part = first_rest.astype(jnp.bfloat16)
    low_part = (first_rest - middle_part.astype(jnp.float32)).astype(jnp.bfloat16)
    return jnp.concatenate([high_part, middle_part, low_part], axis=0)


def bead_forces(
    feature_table,
    coordinate_table,
    neighbours,
    images,
    w_query,
    w_key,
    w_value,
    w_probe,
    radial_rate,
):
    near_count, atom_count = neighbours.shape
    table_rows, channels = feature_table.shape
    head_count = radial_rate.shape[0]
    head_size = channels // head_count
    probe_mats = probe_matrices(
        feature_table[:atom_count], w_query, w_key, w_value, w_probe, head_count
    )
    coordinate_pieces = split_pieces(coordinate_table)
    own_coords = coordinate_table[:, :atom_count]
    shift_table = image_offsets(images)
    block_size = min(atom_count, 128)
    block_count = atom_count // block_size
    table_index = jnp.arange(table_rows, dtype=jnp.int32)

    def one_block(block_id):
        selector = (
            neighbours.reshape(near_count * block_size)[:, None] == table_index[None, :]
        ).astype(jnp.bfloat16)
        picked = jnp.dot(selector, feature_table, preferred_element_type=jnp.float32).astype(
            jnp.bfloat16
        )
        gathered = picked.reshape(near_count, block_size, channels)
        picked_pieces = jnp.einsum(
            "pr,mr->pm", coordinate_pieces, selector, preferred_element_type=jnp.float32
        )
        picked_pieces = picked_pieces.reshape(3, 3, near_count, block_size)
        near_coords = picked_pieces[0] + picked_pieces[1] + picked_pieces[2]
        block_offsets = near_coords - own_coords[:, None, :] + shift_table
        pair_terms = jnp.einsum(
            "kac,aec->eka", gathered, probe_mats, preferred_element_type=jnp.float32
        )
        return attend_forces(pair_terms, block_offsets, radial_rate, head_size)

    blocks = lax.map(one_block, jnp.arange(block_count))
    return blocks.transpose(1, 0, 2).reshape(3, atom_count)


def body(
    positions,
    momenta,
    masses,
    features,
    neighbours,
    images,
    face_map,
    w_query,
    w_key,
    w_value,
    w_probe,
    radial_rate,
):
    bead_local = positions.shape[0]
    atom_count = masses.shape[0]
    send_rows = jnp.concatenate([face_map[0, 0], face_map[1, 0]])
    atom_index = jnp.arange(atom_count, dtype=jnp.int32)
    row_select = send_rows[:, None] == atom_index[None, :]
    feature_buffer = jnp.einsum(
        "ra,bac->brc", row_select.astype(jnp.bfloat16), features, preferred_element_type=jnp.float32
    ).astype(jnp.bfloat16)
    coordinate_buffer = jnp.einsum(
        "bca,ra->bcr", positions, row_select.astype(jnp.float32), precision=lax.Precision.HIGHEST
    )
    force_list = []
    feature_halo = padded(feature_buffer, (("space", 1),), atom_count)
    coordinate_halo = padded(coordinate_buffer, (("space", 2),), atom_count)
    for bead_slot in range(bead_local):
        feature_table = jnp.concatenate(
            [
                features[bead_slot],
                feature_halo[bead_slot, :atom_count],
                feature_halo[bead_slot, 3 * atom_count :],
            ],
            axis=0,
        )
        coordinate_table = jnp.concatenate(
            [
                positions[bead_slot],
                coordinate_halo[bead_slot, :, :atom_count],
                coordinate_halo[bead_slot, :, 3 * atom_count :],
            ],
            axis=1,
        )
        force_list.append(
            bead_forces(
                feature_table,
                coordinate_table,
                neighbours,
                images,
                w_query,
                w_key,
                w_value,
                w_probe,
                radial_rate,
            )
        )
    kicked = momenta + jnp.stack(force_list)
    bead_groups = lax.axis_size("bead")
    bead_count = bead_local * bead_groups
    transform = mode_table(bead_count)
    frequency = frequencies(bead_count)
    stacked = jnp.stack([positions, kicked])
    group_id = lax.axis_index("bead")
    own_columns = lax.dynamic_slice_in_dim(transform, group_id * bead_local, bead_local, 1)
    own_frequency = lax.dynamic_slice_in_dim(frequency, group_id * bead_local, bead_local)
    own_bead_rows = lax.dynamic_slice_in_dim(transform, group_id * bead_local, bead_local, 0)
    coeffs = own_columns
    mode_parts = jnp.einsum(
        "bk,sbcn->skcn",
        coeffs,
        gathered_copies(stacked, "bead", 1),
        precision=lax.Precision.HIGHEST,
    )
    next_pos, next_mom = propagate(mode_parts[0], mode_parts[1], masses, own_frequency)
    coeffs = own_bead_rows
    result = jnp.einsum(
        "bk,skcn->sbcn",
        coeffs,
        gathered_copies(jnp.stack([next_pos, next_mom]), "bead", 1),
        precision=lax.Precision.HIGHEST,
    )
    return (result[0], result[1])


def solution(mesh):
    placed = (
        P("bead", None, "space"),
        P("bead", None, "space"),
        P("space"),
        P("bead", "space", None),
        P(None, "space"),
        P(None, "space"),
        P(None, "space", None),
        P(),
        P(),
        P(),
        P(),
        P(),
    )
    return jax.shard_map(
        body,
        mesh=mesh,
        in_specs=placed,
        out_specs=(P("bead", None, "space"), P("bead", None, "space")),
        check_vma=False,
    )
```

profile of v0, /device:TPU:2, one launch (start us, length us, event | category | flops | bytes accessed | tf_op | source)
XLA Modules:
  0.0 100.4 jit_solution(10940423617225056439)
XLA Ops:
  0.7 0.7 slice_bitcast_fusion.23
  1.4 0.9 convolution_bitcast_fusion.2
  2.4 13.3 %collective-permute-start.3 = (f32[4,3,128]{2,0,1:T(4,128)S(1)}, f32[4,3,128]{2,0,1:T(4,128)S(1)}, u32[]{:S(2)}, u32[]{:S(2)}) collective-permute-start(f32[4,3,128]{2,0,1:T(4,128)S(1)} %get-tuple-element.149), channel_id=1, source_target_pairs={{8,0},{16,8},{24,16},{32,24},{40,32},{48,40},{56,48},{64,56},{72,6... | collective-permute-start | bytes 18440 | tf_op jit(solution)/shard_map/ppermute | solution.py:20
  15.7 1.9 %collective-permute-start.2 = (f32[4,3,128]{2,1,0:T(4,128)S(1)}, f32[4,3,128]{2,1,0:T(4,128)S(1)}, u32[]{:S(2)}, u32[]{:S(2)}) collective-permute-start(f32[4,3,128]{2,1,0:T(4,128)S(1)} %copy.123), channel_id=1, source_target_pairs={{0,8},{8,16},{16,24},{24,32},{32,40},{40,48},{48,56},{56,64},{64,7... | collective-permute-start | bytes 18440 | tf_op jit(solution)/shard_map/ppermute | solution.py:17
  17.6 1.2 %fusion.52 = bf16[4,256,128]{2,1,0:T(8,128)(2,1)S(1)} fusion(bf16[4,128,128]{2,1,0:T(8,128)(2,1)} %param.15, s32[256]{0:T(256)S(1)} %pad_add_fusion), kind=kOutput, calls=%fused_computation.54 | convolution fusion | flops 33718272 | bytes 394240 | tf_op jit(solution)/shard_map/ra,bac->brc/dot_general | solution.py:186
  18.8 0.7 fusion.252
  19.5 7.8 %collective-permute-start.1 = (bf16[4,128,128]{2,1,0:T(8,128)(2,1)}, bf16[4,128,128]{2,1,0:T(8,128)(2,1)S(1)}, u32[]{:S(2)}, u32[]{:S(2)}) collective-permute-start(bf16[4,128,128]{2,1,0:T(8,128)(2,1)} %get-tuple-element.106), channel_id=1, source_target_pairs={{8,0},{16,8},{24,16},{32,24},{40,32},{48,40},{56,48},{64,56},{72,6... | collective-permute-start | bytes 393224 | tf_op jit(solution)/shard_map/ppermute | solution.py:20
  27.4 1.9 %collective-permute-start = (bf16[4,128,128]{2,1,0:T(8,128)(2,1)}, bf16[4,128,128]{2,1,0:T(8,128)(2,1)S(1)}, u32[]{:S(2)}, u32[]{:S(2)}) collective-permute-start(bf16[4,128,128]{2,1,0:T(8,128)(2,1)} %get-tuple-element.105), channel_id=1, source_target_pairs={{0,8},{8,16},{16,24},{24,32},{32,40},{40,48},{48,56},{56,64},{64,7... | collective-permute-start | bytes 393224 | tf_op jit(solution)/shard_map/ppermute | solution.py:17
  29.3 0.7 copy.178
  30.0 1.4 %slice_bitcast_fusion.9 = (bf16[128,128]{1,0:T(8,128)(2,1)}, bf16[128,128]{1,0:T(8,128)(2,1)}, bf16[128,128]{1,0:T(8,128)(2,1)S(1)}, bf16[128,128]{1,0:T(8,128)(2,1)}) fusion(bf16[4,128,128]{2,1,0:T(8,128)(2,1)} %param.15), kind=kLoop, calls=%fused_computation.227 | loop fusion | bytes 262144 | tf_op jit(solution)/shard_map/squeeze | solution.py:198
  31.4 0.9 copy.88
  32.3 0.9 fusion.172
  33.2 0.9 fusion.168
  34.1 0.9 copy.86
  35.0 0.9 fusion.174
  35.9 0.9 fusion.170
  36.8 0.9 fusion.164
  37.7 0.1 fusion.166
  37.9 0.2 fusion.160
  38.0 0.2 fusion.162
  38.5 0.1 copy.89
  38.6 0.1 copy.87
  38.7 0.6 fusion.54
  39.3 0.6 fusion.56
  39.9 0.6 fusion.53
  40.5 0.6 fusion.55
  41.1 0.6 fusion.58
  41.7 0.6 fusion.57
  42.3 0.6 fusion.60
  42.9 0.6 fusion.59
  43.5 0.7 fusion.251
  44.5 0.7 multiply_multiply_fusion.2
  45.2 0.1 fusion.190
  45.6 2.3 %fusion.10 = f32[9,8192]{1,0:T(8,128)S(1)} fusion(s32[8192]{0:T(1024)S(1)} %bitcast.318, bf16[3,384]{1,0:T(4,128)(2,1)S(1)} %get-tuple-element.177, bf16[3,384]{1,0:T(4,128)(2,1)S(1)} %get-tuple-element.176, bf16[3,384]{1,0:T(4,128)(2,1)S(1)} %get-tuple-element.195), kind=kOutput, calls=%fused_computation.11 | convolution fusion | flops 59789568 | bytes 334592 | tf_op jit(solution)/shard_map/while/body/eval_jaxpr/pr,mr->pm/dot_general | solution.py:152
  47.9 2.3 %fusion.8 = f32[9,8192]{1,0:T(8,128)S(1)} fusion(s32[8192]{0:T(1024)S(1)} %bitcast.319, bf16[3,384]{1,0:T(4,128)(2,1)S(1)} %get-tuple-element.188, bf16[3,384]{1,0:T(4,128)(2,1)S(1)} %get-tuple-element.189, bf16[3,384]{1,0:T(4,128)(2,1)S(1)} %get-tuple-element.194), kind=kOutput, calls=%fused_computation.9 | convolution fusion | flops 59789568 | bytes 334592 | tf_op jit(solution)/shard_map/while/body/eval_jaxpr/pr,mr->pm/dot_general | solution.py:152
  50.2 0.4 fusion.116
  50.7 0.1 copy.101
  50.8 2.4 %fusion.6 = f32[9,8192]{1,0:T(8,128)S(1)} fusion(s32[8192]{0:T(1024)S(1)} %bitcast.320, bf16[3,384]{1,0:T(4,128)(2,1)S(1)} %get-tuple-element.179, bf16[3,384]{1,0:T(4,128)(2,1)S(1)} %get-tuple-element.178, bf16[3,384]{1,0:T(4,128)(2,1)S(1)} %get-tuple-element.193), kind=kOutput, calls=%fused_computation.7 | convolution fusion | flops 59789568 | bytes 334592 | tf_op jit(solution)/shard_map/while/body/eval_jaxpr/pr,mr->pm/dot_general | solution.py:152
  53.3 2.3 %fusion.4 = f32[9,8192]{1,0:T(8,128)S(1)} fusion(s32[8192]{0:T(1024)S(1)} %bitcast.321, bf16[3,384]{1,0:T(4,128)(2,1)S(1)} %get-tuple-element.190, bf16[3,384]{1,0:T(4,128)(2,1)S(1)} %get-tuple-element.191, bf16[3,384]{1,0:T(4,128)(2,1)S(1)} %get-tuple-element.192), kind=kOutput, calls=%fused_computation.5 | convolution fusion | flops 59789568 | bytes 334592 | tf_op jit(solution)/shard_map/while/body/eval_jaxpr/pr,mr->pm/dot_general | solution.py:152
  55.5 0.4 fusion.110
  56.1 0.1 copy.112
  56.2 2.9 %fusion.12 = bf16[8192,128]{1,0:T(8,128)(2,1)S(1)} fusion(s32[8192]{0:T(1024)S(1)} %bitcast.322, bf16[128,128]{1,0:T(8,128)(2,1)S(1)} %get-tuple-element.128, bf16[128,128]{1,0:T(8,128)(2,1)S(1)} %get-tuple-element.124, bf16[128,128]{1,0:T(8,128)(2,1)S(1)} %get-tuple-element.109), kind=kOutput, calls=%fused_computation.13 | convolution fusion | flops 809795584 | bytes 2228224 | tf_op jit(solution)/shard_map/while/body/eval_jaxpr/dot_general | solution.py:148
  59.2 1.8 %fusion.32 = f32[16,64,128]{1,0,2:T(8,128)S(1)} fusion(bf16[64,128,128]{2,1,0:T(8,128)(2,1)S(1)} %bitcast.269, bf16[128,16,128]{2,0,1:T(8,128)(2,1)S(1)} %pad_maximum_fusion), kind=kOutput, calls=%fused_computation.33 | convolution fusion | flops 33554432 | bytes 3145728 | tf_op jit(solution)/shard_map/while/body/eval_jaxpr/kac,aec->eka/dot_general | solution.py:158
  61.0 0.4 fusion.255
  61.5 0.3 copy-done.16
  61.8 2.9 %fusion.13 = bf16[8192,128]{1,0:T(8,128)(2,1)S(1)} fusion(s32[8192]{0:T(1024)S(1)} %bitcast.323, bf16[128,128]{1,0:T(8,128)(2,1)S(1)} %get-tuple-element.127, bf16[128,128]{1,0:T(8,128)(2,1)S(1)} %get-tuple-element.123, bf16[128,128]{1,0:T(8,128)(2,1)S(1)} %copy-done.16), kind=kOutput, calls=%fused_computation.14 | convolution fusion | flops 809795584 | bytes 2228224 | tf_op jit(solution)/shard_map/while/body/eval_jaxpr/dot_general | solution.py:148
  64.7 1.8 %fusion.35 = f32[16,64,128]{1,0,2:T(8,128)S(1)} fusion(bf16[64,128,128]{2,1,0:T(8,128)(2,1)S(1)} %bitcast.270, bf16[128,16,128]{2,0,1:T(8,128)(2,1)S(1)} %pad_maximum_fusion.1), kind=kOutput, calls=%fused_computation.34 | convolution fusion | flops 33554432 | bytes 3145728 | tf_op jit(solution)/shard_map/while/body/eval_jaxpr/kac,aec->eka/dot_general | solution.py:158
  66.5 0.4 fusion.256
  67.0 0.3 copy-done.15
  67.3 2.9 %fusion.14 = bf16[8192,128]{1,0:T(8,128)(2,1)S(1)} fusion(s32[8192]{0:T(1024)S(1)} %bitcast.324, bf16[128,128]{1,0:T(8,128)(2,1)S(1)} %get-tuple-element.125, bf16[128,128]{1,0:T(8,128)(2,1)S(1)} %get-tuple-element.121, bf16[128,128]{1,0:T(8,128)(2,1)S(1)} %copy-done.15), kind=kOutput, calls=%fused_computation.15 | convolution fusion | flops 809795584 | bytes 2228224 | tf_op jit(solution)/shard_map/while/body/eval_jaxpr/dot_general | solution.py:148
  70.2 1.8 %fusion.38 = f32[16,64,128]{1,0,2:T(8,128)S(1)} fusion(bf16[64,128,128]{2,1,0:T(8,128)(2,1)S(1)} %bitcast.271, bf16[128,16,128]{2,0,1:T(8,128)(2,1)S(1)} %pad_maximum_fusion.2), kind=kOutput, calls=%fused_computation.35 | convolution fusion | flops 33554432 | bytes 3145728 | tf_op jit(solution)/shard_map/while/body/eval_jaxpr/kac,aec->eka/dot_general | solution.py:158
  72.1 0.4 fusion.257
  72.5 0.3 copy-done.14
  72.8 3.1 %fusion.15 = bf16[8192,128]{1,0:T(8,128)(2,1)S(1)} fusion(s32[8192]{0:T(1024)S(1)} %bitcast.325, bf16[128,128]{1,0:T(8,128)(2,1)S(1)} %get-tuple-element.126, bf16[128,128]{1,0:T(8,128)(2,1)S(1)} %get-tuple-element.122, bf16[128,128]{1,0:T(8,128)(2,1)S(1)} %copy-done.14), kind=kOutput, calls=%fused_computation.16 | convolution fusion | flops 809795584 | bytes 2228224 | tf_op jit(solution)/shard_map/while/body/eval_jaxpr/dot_general | solution.py:148
  76.0 1.8 %fusion.41 = f32[16,64,128]{1,0,2:T(8,128)S(1)} fusion(bf16[64,128,128]{2,1,0:T(8,128)(2,1)S(1)} %bitcast.272, bf16[128,16,128]{2,0,1:T(8,128)(2,1)S(1)} %pad_maximum_fusion.3), kind=kOutput, calls=%fused_computation.36 | convolution fusion | flops 33554432 | bytes 3145728 | tf_op jit(solution)/shard_map/while/body/eval_jaxpr/kac,aec->eka/dot_general | solution.py:158
  77.9 0.4 fusion.258
  78.4 0.1 copy-done.4
  78.7 0.7 broadcast_in_dim.85
  79.3 5.7 %all-to-all-start = ((f32[8,2,4,3,128]{4,2,3,1,0:T(4,128)}), f32[8,2,4,3,128]{4,2,3,1,0:T(4,128)S(1)}, u32[]{:S(2)}, u32[]{:S(2)}) async-start(f32[8,2,4,3,128]{4,2,3,1,0:T(4,128)} %broadcast_in_dim.85), calls=%async_computation | async-start | bytes 196608 | tf_op jit(solution)/shard_map/all_to_all | solution.py:27
  85.1 5.0 %all-to-all-done = f32[8,2,4,3,128]{4,2,3,1,0:T(4,128)S(1)} async-done(((f32[8,2,4,3,128]{4,2,3,1,0:T(4,128)}), f32[8,2,4,3,128]{4,2,3,1,0:T(4,128)S(1)}, u32[]{:S(2)}, u32[]{:S(2)}) %all-to-all-start) | async-done | bytes 98336 | tf_op jit(solution)/shard_map/all_to_all | solution.py:27
  90.1 0.2 convolution_bitcast_fusion.1
  90.4 9.1 %all_to_all.10 = f32[8,2,4,3,128]{4,2,3,1,0:T(4,128)S(1)} all-to-all(f32[8,2,4,3,128]{4,2,3,1,0:T(4,128)S(1)} %broadcast_in_dim.87), channel_id=1, replica_groups=mesh['space'=64,'bead'=8] {'bead'}, dimensions={0} | all-to-all | bytes 196608 | tf_op jit(solution)/shard_map/all_to_all | solution.py:27
  99.5 0.3 convolution_bitcast_fusion
  99.8 0.6 slice_bitcast_fusion.12
  (107 shorter events, 1.5 us)
Async XLA Ops:
  0.6 37.1 %copy-start = (bf16[4,128,128]{2,1,0:T(8,128)(2,1)S(1)}, bf16[4,128,128]{2,1,0:T(8,128)(2,1)}, u32[]{:S(2)}) copy-start(bf16[4,128,128]{2,1,0:T(8,128)(2,1)} %param.15) | copy-start | bytes 393220
  0.6 37.7 %copy-start.11 = (s32[64,128]{1,0:T(8,128)S(1)}, s32[64,128]{1,0:T(8,128)}, u32[]{:S(2)}) copy-start(s32[64,128]{1,0:T(8,128)} %param.17) | copy-start | bytes 98308
  0.7 37.8 %copy-start.12 = (bf16[128,128]{1,0:T(8,128)(2,1)S(1)}, bf16[128,128]{1,0:T(8,128)(2,1)}, u32[]{:S(2)}) copy-start(bf16[128,128]{1,0:T(8,128)(2,1)} %param.21) | copy-start | bytes 98308
  0.7 37.9 %copy-start.13 = (bf16[128,128]{1,0:T(8,128)(2,1)S(1)}, bf16[128,128]{1,0:T(8,128)(2,1)}, u32[]{:S(2)}) copy-start(bf16[128,128]{1,0:T(8,128)(2,1)} %param.20) | copy-start | bytes 98308
  2.4 43.0 %collective-permute-start.3 = (f32[4,3,128]{2,0,1:T(4,128)S(1)}, f32[4,3,128]{2,0,1:T(4,128)S(1)}, u32[]{:S(2)}, u32[]{:S(2)}) collective-permute-start(f32[4,3,128]{2,0,1:T(4,128)S(1)} %get-tuple-element.149), channel_id=1, source_target_pairs={{8,0},{16,8},{24,16},{32,24},{40,32},{48,40},{56,48},{64,56},{72,6... | collective-permute-start | bytes 18440 | tf_op jit(solution)/shard_map/ppermute | solution.py:20
  15.7 29.8 %collective-permute-start.2 = (f32[4,3,128]{2,1,0:T(4,128)S(1)}, f32[4,3,128]{2,1,0:T(4,128)S(1)}, u32[]{:S(2)}, u32[]{:S(2)}) collective-permute-start(f32[4,3,128]{2,1,0:T(4,128)S(1)} %copy.123), channel_id=1, source_target_pairs={{0,8},{8,16},{16,24},{24,32},{32,40},{40,48},{48,56},{56,64},{64,7... | collective-permute-start | bytes 18440 | tf_op jit(solution)/shard_map/ppermute | solution.py:17
  19.5 36.7 %collective-permute-start.1 = (bf16[4,128,128]{2,1,0:T(8,128)(2,1)}, bf16[4,128,128]{2,1,0:T(8,128)(2,1)S(1)}, u32[]{:S(2)}, u32[]{:S(2)}) collective-permute-start(bf16[4,128,128]{2,1,0:T(8,128)(2,1)} %get-tuple-element.106), channel_id=1, source_target_pairs={{8,0},{16,8},{24,16},{32,24},{40,32},{48,40},{56,48},{64,56},{72,6... | collective-permute-start | bytes 393224 | tf_op jit(solution)/shard_map/ppermute | solution.py:20
  27.4 28.8 %collective-permute-start = (bf16[4,128,128]{2,1,0:T(8,128)(2,1)}, bf16[4,128,128]{2,1,0:T(8,128)(2,1)S(1)}, u32[]{:S(2)}, u32[]{:S(2)}) collective-permute-start(bf16[4,128,128]{2,1,0:T(8,128)(2,1)} %get-tuple-element.105), channel_id=1, source_target_pairs={{0,8},{8,16},{16,24},{24,32},{32,40},{40,48},{48,56},{56,64},{64,7... | collective-permute-start | bytes 393224 | tf_op jit(solution)/shard_map/ppermute | solution.py:17
  30.0 8.3 %copy-start.1 = (f32[4,3,128]{2,1,0:T(4,128)}, f32[4,3,128]{2,1,0:T(4,128)S(1)}, u32[]{:S(2)}) copy-start(f32[4,3,128]{2,1,0:T(4,128)S(1)} %copy.178) | copy-start | bytes 18436
  38.3 7.1 %copy-start.3 = (f32[3,128]{1,0:T(4,128)}, f32[3,128]{1,0:T(4,128)S(1)}, u32[]{:S(2)}) copy-start(f32[3,128]{1,0:T(4,128)S(1)} %get-tuple-element.164) | copy-start | bytes 4612
  38.3 7.1 %copy-start.7 = (f32[3,128]{1,0:T(4,128)}, f32[3,128]{1,0:T(4,128)S(1)}, u32[]{:S(2)}) copy-start(f32[3,128]{1,0:T(4,128)S(1)} %get-tuple-element.166) | copy-start | bytes 4612
  38.4 7.2 %copy-start.5 = (f32[3,128]{1,0:T(4,128)}, f32[3,128]{1,0:T(4,128)S(1)}, u32[]{:S(2)}) copy-start(f32[3,128]{1,0:T(4,128)S(1)} %get-tuple-element.165) | copy-start | bytes 4612
  38.4 7.2 %copy-start.9 = (f32[3,128]{1,0:T(4,128)}, f32[3,128]{1,0:T(4,128)S(1)}, u32[]{:S(2)}) copy-start(f32[3,128]{1,0:T(4,128)S(1)} %get-tuple-element.167) | copy-start | bytes 4612
  42.3 2.2 %copy-start.19 = (f32[128]{0:T(128)S(1)}, f32[128]{0:T(128)}, u32[]{:S(2)}) copy-start(f32[128]{0:T(128)} %param.14) | copy-start | bytes 1540
  44.2 0.9 copy-start.22
  44.3 0.9 copy-start.24
  44.3 1.3 %copy-start.26 = (s32[64,128]{1,0:T(8,128)S(1)}, s32[64,128]{1,0:T(8,128)}, u32[]{:S(2)}) copy-start(s32[64,128]{1,0:T(8,128)} %param.16) | copy-start | bytes 98308
  47.9 2.9 %copy-start.27 = (s32[64,128]{1,0:T(8,128)S(1)}, s32[64,128]{1,0:T(8,128)}, u32[]{:S(2)}) copy-start(s32[64,128]{1,0:T(8,128)} %param.16) | copy-start | bytes 98308
  59.2 1.9 %copy-start.28 = (f32[8]{0:T(128)S(1)}, f32[8]{0:T(128)}, u32[]{:S(2)}) copy-start(f32[8]{0:T(128)} %param.23) | copy-start | bytes 100
  61.0 0.8 copy-start.16
  66.5 0.8 copy-start.15
  72.1 0.8 copy-start.14
  77.8 0.7 copy-start.4
  77.8 0.7 copy-start.6
  77.8 0.7 copy-start.8
  77.8 0.7 copy-start.10
  77.8 0.8 copy-start.18
  77.8 0.8 copy-start.2
  77.8 7.2 %copy-start.23 = (f32[4]{0:T(128)S(1)}, f32[4]{0:T(128)}, u32[]{:S(2)}) copy-start(f32[4]{0:T(128)} %copy-done.22) | copy-start | bytes 52
  77.8 7.2 %copy-start.25 = (f32[4]{0:T(128)S(1)}, f32[4]{0:T(128)}, u32[]{:S(2)}) copy-start(f32[4]{0:T(128)} %copy-done.24) | copy-start | bytes 52
  77.9 12.4 %copy-start.17 = (f32[4,128]{1,0:T(4,128)S(1)}, f32[4,128]{1,0:T(4,128)}, u32[]{:S(2)}) copy-start(f32[4,128]{1,0:T(4,128)} %multiply_multiply_fusion.2) | copy-start | bytes 6148
  77.9 12.4 %copy-start.20 = (f32[128]{0:T(128)S(1)}, f32[128]{0:T(128)}, u32[]{:S(2)}) copy-start(f32[128]{0:T(128)} %param.14) | copy-start | bytes 1540
  77.9 12.4 %copy-start.21 = (f32[4]{0:T(128)S(1)}, f32[4]{0:T(128)}, u32[]{:S(2)}) copy-start(f32[4]{0:T(128)} %get-tuple-element.89) | copy-start | bytes 52
  79.3 10.7 %all-to-all-start = ((f32[8,2,4,3,128]{4,2,3,1,0:T(4,128)}), f32[8,2,4,3,128]{4,2,3,1,0:T(4,128)S(1)}, u32[]{:S(2)}, u32[]{:S(2)}) async-start(f32[8,2,4,3,128]{4,2,3,1,0:T(4,128)} %broadcast_in_dim.85), calls=%async_computation | async-start | bytes 196608 | tf_op jit(solution)/shard_map/all_to_all | solution.py:27
where the time goes:
time: 102 us; the launch traced here: 100 us
  matrix products  40.8 us (40%)
  starting transfers between devices  30.7 us (30%)
  local copies, waits for them, and re-layouts  9.48 us (9%)
  blocking collectives  9.07 us (9%)
  waiting for transfers between devices  4.97 us (5%)
  other arithmetic  3.87 us (4%)
  between operations  1.5 us (1%)
    ppermute x2, starting transfers between devices, padded(): lax.ppermute(lax.slice_in_dim(block, 0, width, axis=dim), axis, backward)  21.1 us
    dot_general x4, matrix products, one_block(): jnp.dot(selector, feature_table, preferred_element_type=jnp.float32)  11.8 us
    dot_general x4, matrix products, one_block(): jnp.einsum('pr,mr->pm', coordinate_pieces, selector, preferred_element_ty...  9.27 us
    all_to_all x1, blocking collectives, from_everyone(): lax.all_to_all(jnp.broadcast_to(x[None], (length, *x.shape)), axis, 0, 0,...  9.07 us
    dot_general x4, matrix products, one_block(): jnp.einsum('kac,aec->eka', gathered, probe_mats, preferred_element_type=j...  7.38 us
    all_to_all x1, starting transfers between devices, from_everyone(): lax.all_to_all(jnp.broadcast_to(x[None], (length, *x.shape)), axis, 0, 0,...  5.74 us
    all_to_all x1, waiting for transfers between devices, from_everyone(): lax.all_to_all(jnp.broadcast_to(x[None], (length, *x.shape)), axis, 0, 0,...  4.96 us
    unnamed x70, local copies, waits for them, and re-layouts  3.84 us
  transfers between devices with their start and end apart: 5, of which 1 were waited for; matrix products, arithmetic and copies ran while one was open for 28% of the time, Pallas kernels for 0%

commit v1 on v0

v1 whole, which is shorter than its diff:
```python
import jax
import jax.numpy as jnp
import numpy as np
from jax import lax
from jax.experimental import pallas as pl
from jax.experimental.pallas import tpu as pltpu
from jax.sharding import PartitionSpec as P

STIFFNESS = 1.3
BOX_LENGTH = 2.0
SCORE_CAP = 30.0
HEADS = 8
EXTRA = 16

F32 = jnp.float32
BF16 = jnp.bfloat16
NT = (((1,), (1,)), ((), ()))
NN = (((1,), (0,)), ((), ()))


def dot(a, b, dims=NN):
    return lax.dot_general(a, b, dims, preferred_element_type=F32)


def halves(x):
    high = x.astype(BF16)
    low = (x - high.astype(F32)).astype(BF16)
    return high, low


def bead_maps(bead_count, groups):
    bead = np.arange(bead_count, dtype=np.float64)[:, None]
    mode = np.arange(bead_count)[None, :]
    angle = 2.0 * np.pi * bead * mode / bead_count
    wave = np.sqrt(2.0 / bead_count)
    flat = np.sqrt(1.0 / bead_count)
    half = bead_count // 2
    table = np.where(mode < half, wave * np.cos(angle), wave * np.sin(angle))
    table = np.where(mode == half, flat * np.cos(angle), table)
    table = np.where(mode == 0, flat, table)
    turn = 2.0 * STIFFNESS * np.sin(np.pi * np.arange(bead_count) / bead_count)
    gain = np.where(turn > 0, np.sin(turn) / np.where(turn > 0, turn, 1.0), 1.0)
    keep = (table * np.cos(turn)) @ table.T
    drift = (table * gain) @ table.T
    pull = (table * (turn * np.sin(turn))) @ table.T
    local = bead_count // groups

    def rows(m):
        return m.reshape(groups, local, bead_count)

    of_pos = np.concatenate([rows(keep), rows(pull)], axis=1)
    of_mom = np.concatenate([rows(drift), rows(keep)], axis=1)
    return np.stack([of_pos, of_mom], axis=1).astype(np.float32)


def pack_kernel(features, positions, face_map, out):
    beads, atoms, _ = features.shape
    for b in range(beads):
        out[b, :atoms, :] = features[b]
        p = positions[:, b, :]
        high = p.astype(BF16)
        rest = p - high.astype(F32)
        mid = rest.astype(BF16)
        low = (rest - mid.astype(F32)).astype(BF16)
        maps = jnp.concatenate([face_map[0], face_map[1]], axis=0).astype(F32).astype(BF16)
        fill = jnp.zeros((EXTRA - 11, atoms), BF16)
        out[b, atoms:, :] = jnp.concatenate([high, mid, low, maps, fill], axis=0)


def pair_lanes(a, b):
    lane = lax.broadcasted_iota(jnp.int32, a.shape, 1)
    return jnp.where(lane < a.shape[1] // 2, a, b)


def lanes_of(x, index):
    return jnp.take_along_axis(x, index, axis=1, mode="promise_in_bounds")


def doubled(x):
    return jnp.concatenate([x, x], axis=0).T


def own_kernel(features, neighbours, w_query, w_key, w_value, w_probe, probes, values, kp):
    beads, atoms, channels = features.shape
    head_size = channels // HEADS
    x = features[...].reshape(beads * atoms, channels)
    lane = lax.broadcasted_iota(jnp.int32, (channels, channels), 1)
    for which, (w_in, w_out) in enumerate(((w_query, w_key), (w_probe, w_value))):
        q = dot(x, w_in[...])
        q_high, q_low = halves(q)
        q2 = jnp.concatenate([q_high, q_low], axis=1)
        w = w_out[...]
        for h in range(0, HEADS, 2):
            w0 = jnp.where(lane // head_size == h, w, jnp.zeros_like(w))
            w1 = jnp.where(lane // head_size == h + 1, w, jnp.zeros_like(w))
            rhs = jnp.concatenate(
                [jnp.concatenate([w0, w0], axis=1), jnp.concatenate([w1, w1], axis=1)], axis=0
            )
            r = dot(q2, rhs, NT).astype(BF16).reshape(beads, atoms, 2 * channels)
            e = which * HEADS + h
            probes[:, e] = r[:, :, :channels]
            probes[:, e + 1] = r[:, :, channels:]
    index = doubled(neighbours[...]) & (atoms - 1)
    for b in range(beads):
        own = features[b]
        for p in range(HEADS // 2):
            for which in range(2):
                e = which * HEADS + p
                s0 = dot(probes[b, e], own, NT)
                s1 = dot(probes[b, e + HEADS // 2], own, NT)
                values[b, p * 2 + which] = pair_lanes(lanes_of(s0, index), lanes_of(s1, index))


def whole(piece, atoms, b, c):
    r = piece[b, atoms:, :].astype(F32)
    return r[c : c + 1] + r[3 + c : 4 + c] + r[6 + c : 7 + c]


def force_kernel(
    lower, upper, probes, values, neighbours, images, positions, momenta, rate, out
):
    beads = lower.shape[0]
    atoms, channels = probes.shape[2], probes.shape[3]
    head_size = channels // HEADS
    near2 = doubled(neighbours[...])
    image = doubled(images[...])
    slab = near2 // atoms
    index = near2 & (atoms - 1)
    low_map = lower[0, atoms + 10 : atoms + 11, :].astype(F32).astype(jnp.int32)
    up_map = upper[0, atoms + 9 : atoms + 10, :].astype(F32).astype(jnp.int32)
    index_low = lanes_of(jnp.broadcast_to(low_map, index.shape), index)
    index_up = lanes_of(jnp.broadcast_to(up_map, index.shape), index)
    is_own = slab == 0
    is_low = slab == 1
    shift = [
        BOX_LENGTH * (m - 1).astype(F32) for m in (image % 3, image // 3 % 3, image // 9)
    ]
    row = lax.broadcasted_iota(jnp.int32, (atoms, atoms), 0)
    col = lax.broadcasted_iota(jnp.int32, (atoms, atoms), 1)
    half = atoms // 2
    same_half = jnp.where((row < half) == (col < half), 1.0, 0.0).astype(BF16)
    same_half2 = jnp.concatenate([same_half, same_half], axis=0)
    ones = jnp.ones((8, 2 * atoms), BF16)
    lane = lax.broadcasted_iota(jnp.int32, (1, atoms), 1)

    def one_bead(b):
        ghosts = jnp.concatenate([lower[b, :atoms, :], upper[b, :atoms, :]], axis=0)
        offsets = []
        for c in range(3):
            own_row = positions[c, b : b + 1, :]
            near_pos = jnp.where(
                is_own,
                lanes_of(jnp.broadcast_to(own_row, index.shape), index),
                jnp.where(
                    is_low,
                    lanes_of(jnp.broadcast_to(whole(lower, atoms, b, c), index.shape), index_low),
                    lanes_of(jnp.broadcast_to(whole(upper, atoms, b, c), index.shape), index_up),
                ),
            )
            own_col = jnp.broadcast_to(own_row, (atoms, atoms)).T
            offsets.append(near_pos - own_col + shift[c])
        dist = offsets[0] * offsets[0] + offsets[1] * offsets[1] + offsets[2] * offsets[2]

        def slot_values(e, own_value):
            s0 = dot(probes[b, e], ghosts, NT)
            s1 = dot(probes[b, e + HEADS // 2], ghosts, NT)
            from_low = pair_lanes(lanes_of(s0[:, :atoms], index_low), lanes_of(s1[:, :atoms], index_low))
            from_up = pair_lanes(lanes_of(s0[:, atoms:], index_up), lanes_of(s1[:, atoms:], index_up))
            return jnp.where(is_own, own_value, jnp.where(is_low, from_low, from_up))

        total = jnp.zeros((atoms, atoms), F32)
        for p in range(HEADS // 2):
            raw = slot_values(p, values[b, 2 * p])
            strength = slot_values(HEADS + p, values[b, 2 * p + 1])
            rates = jnp.where(lane < half, rate[0, p], rate[0, p + HEADS // 2])
            logit = SCORE_CAP * jnp.tanh(raw * (head_size**-0.5 / SCORE_CAP)) - rates * dist
            weight = jnp.exp(logit)
            w_high, w_low = halves(weight)
            norm = dot(jnp.concatenate([w_high, w_low], axis=1), same_half2)
            total = total + weight / norm * strength
        total = total * (1.0 / (HEADS * head_size**0.5))
        for c in range(3):
            f_high, f_low = halves(total * offsets[c])
            f = dot(ones, jnp.concatenate([f_high, f_low], axis=1), NT)[0:1]
            kicked = momenta[c, b : b + 1, :] + f
            for g in range(out.shape[0]):
                out[g, 1, c, b : b + 1, :] = kicked
                out[g, 0, c, b : b + 1, :] = positions[c, b : b + 1, :]

    for b in range(beads):
        one_bead(b)


def bead_kernel(group, everyone, masses, table, new_pos, new_mom):
    groups, _, _, local, atoms = everyone.shape
    g = group[0]
    of_pos = table[g, 0]
    of_mom = table[g, 1]
    m = masses[...]
    for c in range(3):
        pos = everyone[:, 0, c].reshape(groups * local, atoms)
        mom = everyone[:, 1, c].reshape(groups * local, atoms)
        a = lax.dot_general(of_pos, pos, NN, precision=lax.Precision.HIGHEST, preferred_element_type=F32)
        d = lax.dot_general(of_mom, mom, NN, precision=lax.Precision.HIGHEST, preferred_element_type=F32)
        new_pos[c] = a[:local] + d[:local] / m
        new_mom[c] = d[local:] - m * a[local:]


def vmem(n):
    return [pl.BlockSpec(memory_space=pltpu.VMEM)] * n


SMEM_SPEC = pl.BlockSpec(memory_space=pltpu.SMEM)


def pack(features, positions, face_map):
    beads, atoms, channels = features.shape
    return pl.pallas_call(
        pack_kernel,
        out_shape=jax.ShapeDtypeStruct((beads, atoms + EXTRA, channels), BF16),
        in_specs=vmem(3),
        out_specs=vmem(1)[0],
        name="pack",
    )(features, positions, face_map)


def own_slab(features, neighbours, w_query, w_key, w_value, w_probe):
    beads, atoms, channels = features.shape
    return pl.pallas_call(
        lambda *refs: own_kernel(*refs, None),
        out_shape=(
            jax.ShapeDtypeStruct((beads, 2 * HEADS, atoms, channels), BF16),
            jax.ShapeDtypeStruct((beads, HEADS, atoms, atoms), F32),
        ),
        in_specs=vmem(6),
        out_specs=tuple(vmem(2)),
        name="own_slab",
    )(features, neighbours, w_query, w_key, w_value, w_probe)


def forces(groups, lower, upper, probes, values, neighbours, images, positions, momenta, rate):
    beads = lower.shape[0]
    atoms = probes.shape[2]
    return pl.pallas_call(
        force_kernel,
        out_shape=jax.ShapeDtypeStruct((groups, 2, 3, beads, atoms), F32),
        in_specs=vmem(8) + [SMEM_SPEC],
        out_specs=vmem(1)[0],
        name="forces",
    )(lower, upper, probes, values, neighbours, images, positions, momenta, rate)


def move_beads(group, everyone, masses, table):
    _, _, _, local, atoms = everyone.shape
    return pl.pallas_call(
        bead_kernel,
        out_shape=(jax.ShapeDtypeStruct((3, local, atoms), F32),) * 2,
        in_specs=[SMEM_SPEC] + vmem(3),
        out_specs=tuple(vmem(2)),
        name="bead_maps",
    )(group, everyone, masses, table)


def body(
    positions, momenta, masses, features, neighbours, images, face_map,
    w_query, w_key, w_value, w_probe, radial_rate,
):
    groups = lax.axis_size("bead")
    beads = positions.shape[0]
    slabs = lax.axis_size("space")
    up = [(i, (i + 1) % slabs) for i in range(slabs)]
    down = [(target, source) for source, target in up]
    pos = jnp.transpose(positions, (1, 0, 2))
    mom = jnp.transpose(momenta, (1, 0, 2))
    message = pack(features, pos, face_map)
    lower = lax.ppermute(message, "space", up)
    upper = lax.ppermute(message, "space", down)
    probes, values = own_slab(features, neighbours, w_query, w_key, w_value, w_probe)
    sent = forces(
        groups, lower, upper, probes, values, neighbours, images, pos, mom, radial_rate[None]
    )
    everyone = lax.all_to_all(sent, "bead", 0, 0, tiled=True)
    table = jnp.asarray(bead_maps(beads * groups, groups))
    group = lax.axis_index("bead").astype(jnp.int32)[None]
    new_pos, new_mom = move_beads(group, everyone, masses[None], table)
    return jnp.transpose(new_pos, (1, 0, 2)), jnp.transpose(new_mom, (1, 0, 2))


def solution(mesh):
    placed = (
        P("bead", None, "space"),
        P("bead", None, "space"),
        P("space"),
        P("bead", "space", None),
        P(None, "space"),
        P(None, "space"),
        P(None, "space", None),
        P(), P(), P(), P(), P(),
    )
    return jax.shard_map(
        body,
        mesh=mesh,
        in_specs=placed,
        out_specs=(P("bead", None, "space"), P("bead", None, "space")),
        check_vma=False,
    )
```

time: 102 us -> 48.6 us (0.48); the launches traced: 100 us -> 48.3 us
  matrix products: 40.8 us -> 0 us
  Pallas kernels: 0 us -> 20.4 us
  starting transfers between devices: 30.7 us -> 20.9 us
  blocking collectives: 9.07 us -> 0 us
  local copies, waits for them, and re-layouts: 9.48 us -> 1.32 us
  other arithmetic: 3.87 us -> 0 us
    dot_general x32 -> x0, matrix products: 40.8 us -> none  [the longest x4 11.8 us: one_block(): jnp.dot(selector, feature_table, preferred_element_type=jnp.float32)]
    pallas_call x0 -> x4, Pallas kernels: none -> 20.4 us  [the longest x1 11.2 us: forces(): pl.pallas_call(force_kernel, out_shape=jax.ShapeDtypeStruct((groups, 2, 3...]
    ppermute x4 -> x2, starting transfers between devices: 25 us -> 15.2 us  [the longest x1 13.3 us: body(): upper = lax.ppermute(message, 'space', down)]
    all_to_all x1 -> x0, blocking collectives: 9.07 us -> none  [from_everyone(): lax.all_to_all(jnp.broadcast_to(x[None], (length, *x.shape)), axis, 0, 0,...]
    squeeze x7 -> x0, local copies, waits for them, and re-layouts: 2.81 us -> none  [the longest x1 1.45 us: body(): features[bead_slot]]
    unnamed x70 -> x6, local copies, waits for them, and re-layouts: 3.84 us -> 1.32 us
    div x4 -> x0, other arithmetic: 1.53 us -> none  [attend_forces(): attention = weights / jnp.sum(weights, axis=1, keepdims=True)]
  transfers between devices with their start and end apart: 5 -> 3, of which waited for: 1 -> 1; matrix products, arithmetic and copies ran while one was open for 28% -> 0% of each run, Pallas kernels for 0% -> 12%
where the time goes in v1:
time: 48.6 us; the launch traced here: 48.3 us
  starting transfers between devices  20.9 us (43%)
  Pallas kernels  20.4 us (42%)
  waiting for transfers between devices  4.98 us (10%)
  local copies, waits for them, and re-layouts  1.32 us (3%)
  between operations  0.66 us (1%)
    ppermute x1, starting transfers between devices, body(): upper = lax.ppermute(message, 'space', down)  13.3 us
    pallas_call x1, Pallas kernels, forces(): pl.pallas_call(force_kernel, out_shape=jax.ShapeDtypeStruct((groups, 2, 3...  11.2 us
    pallas_call x1, Pallas kernels, own_slab(): pl.pallas_call(lambda *refs: own_kernel(*refs, None), out_shape=(jax.Shap...  5.87 us
    all_to_all x1, starting transfers between devices, body(): everyone = lax.all_to_all(sent, 'bead', 0, 0, tiled=True)  5.74 us
    all_to_all x1, waiting for transfers between devices, body(): everyone = lax.all_to_all(sent, 'bead', 0, 0, tiled=True)  4.98 us
    ppermute x1, starting transfers between devices, body(): lower = lax.ppermute(message, 'space', up)  1.91 us
    pallas_call x1, Pallas kernels, move_beads(): pl.pallas_call(bead_kernel, out_shape=(jax.ShapeDtypeStruct((3, local, at...  1.73 us
    pallas_call x1, Pallas kernels, pack(): pl.pallas_call(pack_kernel, out_shape=jax.ShapeDtypeStruct((beads, atoms...  1.62 us
  transfers between devices with their start and end apart: 3, of which 1 were waited for; matrix products, arithmetic and copies ran while one was open for 0% of the time, Pallas kernels for 12%

profile of v1, /device:TPU:2, one launch (start us, length us, event | category | flops | bytes accessed | tf_op | source)
XLA Modules:
  0.0 48.3 jit_solution(1548548171884506638)
XLA Ops:
  0.6 1.6 %pack.1 = bf16[4,144,128]{2,1,0:T(8,128)(2,1)} custom-call(bf16[4,128,128]{2,1,0:T(8,128)(2,1)} %refs_0_.1, f32[3,4,128]{2,1,0:T(4,128)} %bitcast.7, s32[2,1,128]{2,1,0:T(1,128)} %face_map.1), custom_call_target="tpu_custom_call" | custom-call | tf_op jit(solution)/shard_map/pack/pallas_call | solution.py:218
  2.3 1.9 %collective-permute-start = (bf16[4,144,128]{2,1,0:T(8,128)(2,1)}, bf16[4,144,128]{2,1,0:T(8,128)(2,1)S(1)}, u32[]{:S(2)}, u32[]{:S(2)}) collective-permute-start(bf16[4,144,128]{2,1,0:T(8,128)(2,1)} %pack.1), channel_id=1, source_target_pairs={{0,8},{8,16},{16,24},{24,32},{32,40},{40,48},{48,56},{56,64},{64,7... | collective-permute-start | bytes 442376 | tf_op jit(solution)/shard_map/ppermute | solution.py:276
  4.2 13.3 %collective-permute-start.1 = (bf16[4,144,128]{2,1,0:T(8,128)(2,1)}, bf16[4,144,128]{2,1,0:T(8,128)(2,1)S(1)}, u32[]{:S(2)}, u32[]{:S(2)}) collective-permute-start(bf16[4,144,128]{2,1,0:T(8,128)(2,1)} %pack.1), channel_id=1, source_target_pairs={{8,0},{16,8},{24,16},{32,24},{40,32},{48,40},{56,48},{64,56},{72,6... | collective-permute-start | bytes 442376 | tf_op jit(solution)/shard_map/ppermute | solution.py:277
  17.5 5.9 %own_slab.1 = (bf16[4,16,128,128]{3,2,1,0:T(8,128)(2,1)}, f32[4,8,128,128]{3,2,1,0:T(8,128)}) custom-call(bf16[4,128,128]{2,1,0:T(8,128)(2,1)} %refs_0_.1, s32[64,128]{1,0:T(8,128)} %neighbours.1, bf16[128,128]{1,0:T(8,128)(2,1)} %refs_2_.1, bf16[128,128]{1,0:T(8,128)(2,1)} %refs_3_.1, bf16[128,128]{1,0:T(8,128)(2,1)} %refs_4_.1, bf16[128,128]{1,0:T(8,128)(2,1)} %refs_5_.1), custom_call_target="tpu_custom_call" | custom-call | tf_op jit(solution)/shard_map/own_slab/pallas_call | solution.py:229
  23.3 0.0 collective-permute-done.lower
  23.3 0.0 copy-start.1
  23.3 0.0 collective-permute-done.1.upper
  23.3 0.0 copy-start.2
  23.4 0.6 %copy-done.1 = bf16[4,144,128]{2,1,0:T(8,128)(2,1)} copy-done((bf16[4,144,128]{2,1,0:T(8,128)(2,1)}, bf16[4,144,128]{2,1,0:T(8,128)(2,1)S(1)}, u32[]{:S(2)}) %copy-start.1) | copy-done | bytes 147480
  24.0 0.1 copy-done.2
  24.0 11.2 %forces.1 = f32[8,2,3,4,128]{4,3,2,1,0:T(4,128)} custom-call(bf16[4,144,128]{2,1,0:T(8,128)(2,1)} %copy-done.1, bf16[4,144,128]{2,1,0:T(8,128)(2,1)} %copy-done.2, bf16[4,16,128,128]{3,2,1,0:T(8,128)(2,1)} %get-tuple-element.6.probes, f32[4,8,128,128]{3,2,1,0:T(8,128)} %get-tuple-element.7.values, s32[64,128]{1,0:T(8,128)} %neighbours.1, s32[64,128]{1,0:T(8,128)} %images.1, ...), custom_call_target="tpu_custom_call" | custom-call | tf_op jit(solution)/shard_map/forces/pallas_call | solution.py:244
  35.2 5.7 %all-to-all-start = ((f32[8,2,3,4,128]{4,3,2,1,0:T(4,128)}), f32[8,2,3,4,128]{4,3,2,1,0:T(4,128)S(1)}, u32[]{:S(2)}, u32[]{:S(2)}) async-start(f32[8,2,3,4,128]{4,3,2,1,0:T(4,128)} %forces.1), calls=%async_computation | async-start | bytes 196608 | tf_op jit(solution)/shard_map/all_to_all | solution.py:282
  41.0 5.0 %all-to-all-done.everyone = f32[8,2,3,4,128]{4,3,2,1,0:T(4,128)S(1)} async-done(((f32[8,2,3,4,128]{4,3,2,1,0:T(4,128)}), f32[8,2,3,4,128]{4,3,2,1,0:T(4,128)S(1)}, u32[]{:S(2)}, u32[]{:S(2)}) %all-to-all-start) | async-done | bytes 98336 | tf_op jit(solution)/shard_map/all_to_all | solution.py:282
  45.9 0.0 copy-start
  46.0 0.6 %copy-done = f32[8,2,3,4,128]{4,3,2,1,0:T(4,128)} copy-done((f32[8,2,3,4,128]{4,3,2,1,0:T(4,128)}, f32[8,2,3,4,128]{4,3,2,1,0:T(4,128)S(1)}, u32[]{:S(2)}) %copy-start) | copy-done | bytes 98328
  46.6 1.7 %bead_maps.1 = (f32[3,4,128]{2,1,0:T(4,128)}, f32[3,4,128]{2,1,0:T(4,128)}) custom-call(s32[1]{0:T(128)} %bitcast.group, f32[8,2,3,4,128]{4,3,2,1,0:T(4,128)} %copy-done, f32[1,128]{1,0:T(1,128)} %bitcast.11, f32[8,2,8,32]{3,2,1,0:T(8,128)} %constant.6.clone.table), custom_call_target="tpu_custom_call" | custom-call | tf_op jit(solution)/shard_map/bead_maps/pallas_call | solution.py:255
Async XLA Ops:
  2.3 21.1 %collective-permute-start = (bf16[4,144,128]{2,1,0:T(8,128)(2,1)}, bf16[4,144,128]{2,1,0:T(8,128)(2,1)S(1)}, u32[]{:S(2)}, u32[]{:S(2)}) collective-permute-start(bf16[4,144,128]{2,1,0:T(8,128)(2,1)} %pack.1), channel_id=1, source_target_pairs={{0,8},{8,16},{16,24},{24,32},{32,40},{40,48},{48,56},{56,64},{64,7... | collective-permute-start | bytes 442376 | tf_op jit(solution)/shard_map/ppermute | solution.py:276
  4.2 19.2 %collective-permute-start.1 = (bf16[4,144,128]{2,1,0:T(8,128)(2,1)}, bf16[4,144,128]{2,1,0:T(8,128)(2,1)S(1)}, u32[]{:S(2)}, u32[]{:S(2)}) collective-permute-start(bf16[4,144,128]{2,1,0:T(8,128)(2,1)} %pack.1), channel_id=1, source_target_pairs={{8,0},{16,8},{24,16},{32,24},{40,32},{48,40},{56,48},{64,56},{72,6... | collective-permute-start | bytes 442376 | tf_op jit(solution)/shard_map/ppermute | solution.py:277
  23.3 0.6 %copy-start.1 = (bf16[4,144,128]{2,1,0:T(8,128)(2,1)}, bf16[4,144,128]{2,1,0:T(8,128)(2,1)S(1)}, u32[]{:S(2)}) copy-start(bf16[4,144,128]{2,1,0:T(8,128)(2,1)S(1)} %collective-permute-done.lower) | copy-start | bytes 442372
  23.3 0.7 %copy-start.2 = (bf16[4,144,128]{2,1,0:T(8,128)(2,1)}, bf16[4,144,128]{2,1,0:T(8,128)(2,1)S(1)}, u32[]{:S(2)}) copy-start(bf16[4,144,128]{2,1,0:T(8,128)(2,1)S(1)} %collective-permute-done.1.upper) | copy-start | bytes 442372
  35.2 10.7 %all-to-all-start = ((f32[8,2,3,4,128]{4,3,2,1,0:T(4,128)}), f32[8,2,3,4,128]{4,3,2,1,0:T(4,128)S(1)}, u32[]{:S(2)}, u32[]{:S(2)}) async-start(f32[8,2,3,4,128]{4,3,2,1,0:T(4,128)} %forces.1), calls=%async_computation | async-start | bytes 196608 | tf_op jit(solution)/shard_map/all_to_all | solution.py:282
  45.9 0.6 %copy-start = (f32[8,2,3,4,128]{4,3,2,1,0:T(4,128)}, f32[8,2,3,4,128]{4,3,2,1,0:T(4,128)S(1)}, u32[]{:S(2)}) copy-start(f32[8,2,3,4,128]{4,3,2,1,0:T(4,128)S(1)} %all-to-all-done.everyone) | copy-start | bytes 294916

commit v2 on v1

v2 whole, which is shorter than its diff:
```python
import jax
import jax.numpy as jnp
import numpy as np
from jax import lax
from jax.experimental import pallas as pl
from jax.experimental.pallas import tpu as pltpu
from jax.sharding import PartitionSpec as P

STIFFNESS = 1.3
BOX_LENGTH = 2.0
SCORE_CAP = 30.0
HEADS = 8
EXTRA = 16
ROWS = 16
STEP = 128
SCOPE = 24 << 20

F32 = jnp.float32
BF16 = jnp.bfloat16
NT = (((1,), (1,)), ((), ()))
NN = (((1,), (0,)), ((), ()))


def dot(a, b, dims=NN):
    return lax.dot_general(a, b, dims, preferred_element_type=F32)


def halves(x):
    high = x.astype(BF16)
    low = (x - high.astype(F32)).astype(BF16)
    return high, low


def bead_maps(bead_count, groups):
    bead = np.arange(bead_count, dtype=np.float64)[:, None]
    mode = np.arange(bead_count)[None, :]
    angle = 2.0 * np.pi * bead * mode / bead_count
    wave = np.sqrt(2.0 / bead_count)
    flat = np.sqrt(1.0 / bead_count)
    half = bead_count // 2
    table = np.where(mode < half, wave * np.cos(angle), wave * np.sin(angle))
    table = np.where(mode == half, flat * np.cos(angle), table)
    table = np.where(mode == 0, flat, table)
    turn = 2.0 * STIFFNESS * np.sin(np.pi * np.arange(bead_count) / bead_count)
    gain = np.where(turn > 0, np.sin(turn) / np.where(turn > 0, turn, 1.0), 1.0)
    keep = (table * np.cos(turn)) @ table.T
    drift = (table * gain) @ table.T
    pull = (table * (turn * np.sin(turn))) @ table.T
    local = bead_count // groups

    def rows(m):
        return m.reshape(groups, local, bead_count)

    of_pos = np.concatenate([rows(keep), rows(pull)], axis=1)
    of_mom = np.concatenate([rows(drift), rows(keep)], axis=1)
    return np.stack([of_pos, of_mom], axis=1).astype(np.float32)


def pack_kernel(features, positions, face_map, out):
    beads, atoms, _ = features.shape
    for b in range(beads):
        out[b, :atoms, :] = features[b]
        p = positions[:, b, :]
        high = p.astype(BF16)
        rest = p - high.astype(F32)
        mid = rest.astype(BF16)
        low = (rest - mid.astype(F32)).astype(BF16)
        maps = jnp.concatenate([face_map[0], face_map[1]], axis=0).astype(F32).astype(BF16)
        fill = jnp.zeros((EXTRA - 11, atoms), BF16)
        out[b, atoms:, :] = jnp.concatenate([high, mid, low, maps, fill], axis=0)


def pair_lanes(a, b):
    lane = lax.broadcasted_iota(jnp.int32, a.shape, 1)
    return jnp.where(lane < a.shape[1] // 2, a, b)


def lanes_of(x, index):
    return jnp.take_along_axis(x, index, axis=1, mode="promise_in_bounds")


def doubled(x):
    return jnp.concatenate([x, x], axis=0).T


def own_kernel(
    features, neighbours, images, positions, w_query, w_key, w_value, w_probe,
    probes, values, base, near,
):
    beads, atoms, channels = features.shape
    head_size = channels // HEADS
    x = features[...].reshape(beads * atoms, channels)
    lane = lax.broadcasted_iota(jnp.int32, (channels, channels), 1)
    for which, (w_in, w_out) in enumerate(((w_query, w_key), (w_probe, w_value))):
        q = dot(x, w_in[...])
        q_high, q_low = halves(q)
        q2 = jnp.concatenate([q_high, q_low], axis=1)
        w = w_out[...]
        for h in range(0, HEADS, 2):
            w0 = jnp.where(lane // head_size == h, w, jnp.zeros_like(w))
            w1 = jnp.where(lane // head_size == h + 1, w, jnp.zeros_like(w))
            rhs = jnp.concatenate(
                [jnp.concatenate([w0, w0], axis=1), jnp.concatenate([w1, w1], axis=1)], axis=0
            )
            r = dot(q2, rhs, NT).astype(BF16).reshape(beads, atoms // ROWS, ROWS, 2 * channels)
            at = (which * HEADS + h) * ROWS
            probes[:, :, at : at + ROWS, :] = r[..., :channels]
            probes[:, :, at + ROWS : at + 2 * ROWS, :] = r[..., channels:]
    near2 = doubled(neighbours[...])
    near[...] = near2
    is_own = near2 < atoms
    index = near2 & (atoms - 1)
    image = images[...]
    plane = lax.div(image, 9)
    rest = image - 9 * plane
    line = lax.div(rest, 3)
    shift = [
        doubled(BOX_LENGTH * (m - 1).astype(F32)) for m in (rest - 3 * line, line, plane)
    ]
    for b in range(beads):
        own = features[b]
        rows = [positions[c, b : b + 1, :] for c in range(3)]
        wide = [jnp.broadcast_to(r, (8, atoms)) for r in rows]
        cols = [jnp.broadcast_to(r, (atoms, atoms)).T for r in rows]
        for g in range(atoms // ROWS):
            s = dot(probes[b, g], own, NT)
            for half in range(0, ROWS, 8):
                lo = g * ROWS + half
                idx = index[lo : lo + 8]
                got = [lanes_of(s[e * ROWS + half : e * ROWS + half + 8], idx) for e in range(2 * HEADS)]
                here = [lanes_of(wide[c], idx) for c in range(3)]
                for p in range(HEADS // 2):
                    for which in range(2):
                        e = which * HEADS + p
                        values[b, 2 * p + which, lo : lo + 8, :] = pair_lanes(got[e], got[e + HEADS // 2])
                for c in range(3):
                    base[b, c, lo : lo + 8, :] = (
                        jnp.where(is_own[lo : lo + 8], here[c], 0.0)
                        - cols[c][lo : lo + 8]
                        + shift[c][lo : lo + 8]
                    )


def whole(piece, atoms, b):
    r = piece[b, atoms:, :].astype(F32)
    return [
        jnp.broadcast_to(r[c : c + 1] + r[3 + c : 4 + c] + r[6 + c : 7 + c], (8, r.shape[1]))
        for c in range(3)
    ]


def force_kernel(
    lower, upper, probes, values, base, near, positions, momenta, rate, out,
    weights, products, forces, raw_scores, picked, indices,
):
    beads = lower.shape[0]
    atoms = values.shape[2]
    channels = probes.shape[3]
    head_size = channels // HEADS
    pairs = HEADS // 2
    near2 = near[...]
    index = near2 & (atoms - 1)
    low_map = lower[0, atoms + 10 : atoms + 11, :].astype(F32).astype(jnp.int32)
    up_map = upper[0, atoms + 9 : atoms + 10, :].astype(F32).astype(jnp.int32)
    indices[0] = lanes_of(jnp.broadcast_to(low_map, index.shape), index)
    indices[1] = lanes_of(jnp.broadcast_to(up_map, index.shape), index)
    row = lax.broadcasted_iota(jnp.int32, (atoms, atoms), 0)
    col = lax.broadcasted_iota(jnp.int32, (atoms, atoms), 1)
    half_lanes = atoms // 2
    same_half = jnp.where((row < half_lanes) == (col < half_lanes), 1.0, 0.0).astype(BF16)
    same_half2 = jnp.concatenate([same_half, same_half], axis=0)
    ones = jnp.ones((8, 2 * atoms), BF16)
    lane = lax.broadcasted_iota(jnp.int32, (8, atoms), 1)
    rates = [jnp.where(lane < half_lanes, rate[0, p], rate[0, p + pairs]) for p in range(pairs)]

    blocks = atoms // STEP
    steps = beads * blocks
    offs = range(0, STEP, 8)

    def scores(i):
        b, q = lax.div(i, blocks), lax.rem(i, blocks)
        ghosts = jnp.concatenate([lower[b, :atoms, :], upper[b, :atoms, :]], axis=0)
        for k in range(STEP // ROWS):
            raw_scores[k] = dot(probes[b, q * (STEP // ROWS) + k], ghosts, NT)

    def select(i):
        b, q = lax.div(i, blocks), lax.rem(i, blocks)
        pos_low = whole(lower, atoms, b)
        pos_up = whole(upper, atoms, b)
        for lo in offs:
            k, half = lo // ROWS, lo % ROWS
            rows = pl.ds(pl.multiple_of(q * STEP + lo, 8), 8)
            n = near[rows, :]
            is_own = n < atoms
            is_low = n < 2 * atoms
            idx_low = indices[0, rows, :]
            idx_up = indices[1, rows, :]
            at = [slice(e * ROWS + half, e * ROWS + half + 8) for e in range(2 * HEADS)]
            from_low = [lanes_of(raw_scores[k, a, :atoms], idx_low) for a in at]
            p_low = [lanes_of(x, idx_low) for x in pos_low]
            from_up = [lanes_of(raw_scores[k, a, atoms:], idx_up) for a in at]
            p_up = [lanes_of(x, idx_up) for x in pos_up]
            ghost = [jnp.where(is_low, l, u) for l, u in zip(from_low, from_up)]
            for c in range(3):
                off = base[b, c, rows, :] + jnp.where(
                    is_own, 0.0, jnp.where(is_low, p_low[c], p_up[c])
                )
                picked[HEADS + c, lo : lo + 8, :] = off
            for which in range(2):
                for p in range(pairs):
                    e = which * HEADS + p
                    picked[2 * p + which, lo : lo + 8, :] = jnp.where(
                        is_own,
                        values[b, 2 * p + which, rows, :],
                        pair_lanes(ghost[e], ghost[e + pairs]),
                    )

    def weigh(i):
        b, q = lax.div(i, blocks), lax.rem(i, blocks)
        whole_block = pl.ds(pl.multiple_of(q * STEP, 8), STEP)
        total = None
        for p in range(pairs):
            for lo in offs:
                here = slice(lo, lo + 8)
                off = [picked[HEADS + c, here, :] for c in range(3)]
                dist = off[0] * off[0] + off[1] * off[1] + off[2] * off[2]
                logit = (
                    SCORE_CAP * jnp.tanh(picked[2 * p, here, :] * (head_size**-0.5 / SCORE_CAP))
                    - rates[p] * dist
                )
                weight = jnp.exp(logit)
                products[p, here, :] = weight * picked[2 * p + 1, here, :]
                weights[p, here, :] = weight
            w_high, w_low = halves(weights[p])
            norm = dot(jnp.concatenate([w_high, w_low], axis=1), same_half2)
            part = products[p] / norm
            total = part if total is None else total + part
        total = total * (1.0 / (HEADS * head_size**0.5))
        for c in range(3):
            forces[b, c, whole_block, :] = total * picked[HEADS + c]

    def finish(b):
        for c in range(3):
            f_high, f_low = halves(forces[b, c])
            f = dot(ones, jnp.concatenate([f_high, f_low], axis=1), NT)[0:1]
            kicked = momenta[c, b : b + 1, :] + f
            for g in range(out.shape[0]):
                out[g, 1, c, b : b + 1, :] = kicked
                out[g, 0, c, b : b + 1, :] = positions[c, b : b + 1, :]

    scores(0)
    select(0)
    scores(1)

    def step(i, carry):
        weigh(i)
        select(i + 1)
        scores(i + 2)
        return carry

    lax.fori_loop(0, steps - 2, step, 0)
    weigh(steps - 2)
    select(steps - 1)
    weigh(steps - 1)
    for b in range(beads):
        finish(b)


def bead_kernel(group, everyone, masses, table, new_pos, new_mom):
    groups, _, _, local, atoms = everyone.shape
    g = group[0]
    of_pos = table[g, 0]
    of_mom = table[g, 1]
    m = masses[...]
    for c in range(3):
        pos = everyone[:, 0, c].reshape(groups * local, atoms)
        mom = everyone[:, 1, c].reshape(groups * local, atoms)
        a = lax.dot_general(of_pos, pos, NN, precision=lax.Precision.HIGHEST, preferred_element_type=F32)
        d = lax.dot_general(of_mom, mom, NN, precision=lax.Precision.HIGHEST, preferred_element_type=F32)
        new_pos[c] = a[:local] + d[:local] / m
        new_mom[c] = d[local:] - m * a[local:]


def vmem(n):
    return [pl.BlockSpec(memory_space=pltpu.VMEM)] * n


SMEM_SPEC = pl.BlockSpec(memory_space=pltpu.SMEM)


def inside(x):
    return pltpu.with_memory_space_constraint(x, pltpu.VMEM)


def outside(x):
    return pltpu.with_memory_space_constraint(x, pltpu.HBM)


def pack(features, positions, face_map):
    beads, atoms, channels = features.shape
    return pl.pallas_call(
        pack_kernel,
        out_shape=pltpu.VMEM((beads, atoms + EXTRA, channels), BF16),
        in_specs=vmem(3),
        out_specs=vmem(1)[0],
        compiler_params=pltpu.CompilerParams(vmem_limit_bytes=SCOPE),
        name="pack",
    )(features, positions, face_map)


def own_slab(features, neighbours, images, positions, *weights):
    beads, atoms, channels = features.shape
    return pl.pallas_call(
        own_kernel,
        out_shape=(
            pltpu.VMEM((beads, atoms // ROWS, 2 * HEADS * ROWS, channels), BF16),
            pltpu.VMEM((beads, HEADS, atoms, atoms), F32),
            pltpu.VMEM((beads, 3, atoms, atoms), F32),
            pltpu.VMEM((atoms, atoms), jnp.int32),
        ),
        in_specs=vmem(8),
        out_specs=tuple(vmem(4)),
        compiler_params=pltpu.CompilerParams(vmem_limit_bytes=SCOPE),
        name="own_slab",
    )(features, neighbours, images, positions, *weights)


def forces(groups, lower, upper, probes, values, base, near, positions, momenta, rate):
    beads = lower.shape[0]
    atoms = values.shape[2]
    return pl.pallas_call(
        force_kernel,
        out_shape=jax.ShapeDtypeStruct((groups, 2, 3, beads, atoms), F32),
        in_specs=vmem(8) + [SMEM_SPEC],
        out_specs=vmem(1)[0],
        scratch_shapes=[
            pltpu.VMEM((HEADS // 2, STEP, atoms), F32),
            pltpu.VMEM((HEADS // 2, STEP, atoms), F32),
            pltpu.VMEM((beads, 3, atoms, atoms), F32),
            pltpu.VMEM((STEP // ROWS, 2 * HEADS * ROWS, 2 * atoms), F32),
            pltpu.VMEM((HEADS + 3, STEP, atoms), F32),
            pltpu.VMEM((2, atoms, atoms), jnp.int32),
        ],
        compiler_params=pltpu.CompilerParams(vmem_limit_bytes=SCOPE),
        name="forces",
    )(*map(inside, (lower, upper, probes, values, base, near)), positions, momenta, rate)


def move_beads(group, everyone, masses, table):
    _, _, _, local, atoms = everyone.shape
    return pl.pallas_call(
        bead_kernel,
        out_shape=(jax.ShapeDtypeStruct((3, local, atoms), F32),) * 2,
        in_specs=[SMEM_SPEC] + vmem(3),
        out_specs=tuple(vmem(2)),
        compiler_params=pltpu.CompilerParams(vmem_limit_bytes=SCOPE),
        name="bead_maps",
    )(group, inside(everyone), outside(masses), outside(table))


def body(
    positions, momenta, masses, features, neighbours, images, face_map,
    w_query, w_key, w_value, w_probe, radial_rate,
):
    groups = lax.axis_size("bead")
    beads = positions.shape[0]
    face_map, features, neighbours, images = map(outside, (face_map, features, neighbours, images))
    w_query, w_key, w_value, w_probe = map(outside, (w_query, w_key, w_value, w_probe))
    slabs = lax.axis_size("space")
    up = [(i, (i + 1) % slabs) for i in range(slabs)]
    down = [(target, source) for source, target in up]
    pos = outside(jnp.transpose(positions, (1, 0, 2)))
    mom = outside(jnp.transpose(momenta, (1, 0, 2)))
    radial_rate = outside(radial_rate[None])
    message = pack(features, pos, face_map)
    upper = lax.ppermute(message, "space", down)
    lower = lax.ppermute(message, "space", up)
    halo_free = own_slab(
        features, neighbours, images, pos, w_query, w_key, w_value, w_probe
    )
    sent = forces(groups, lower, upper, *halo_free, pos, mom, radial_rate)
    everyone = lax.all_to_all(sent, "bead", 0, 0, tiled=True)
    table = jnp.asarray(bead_maps(beads * groups, groups))
    group = lax.axis_index("bead").astype(jnp.int32)[None]
    new_pos, new_mom = move_beads(group, everyone, masses[None], table)
    return jnp.transpose(new_pos, (1, 0, 2)), jnp.transpose(new_mom, (1, 0, 2))


def solution(mesh):
    placed = (
        P("bead", None, "space"),
        P("bead", None, "space"),
        P("space"),
        P("bead", "space", None),
        P(None, "space"),
        P(None, "space"),
        P(None, "space", None),
        P(), P(), P(), P(), P(),
    )
    return jax.shard_map(
        body,
        mesh=mesh,
        in_specs=placed,
        out_specs=(P("bead", None, "space"), P("bead", None, "space")),
        check_vma=False,
    )
```

time: 48.6 us -> 45.1 us (0.928)
  Pallas kernels: 20.4 us -> 12.2 us
  waiting for transfers between devices: 4.98 us -> 11.2 us
  local copies, waits for them, and re-layouts: 1.32 us -> 0 us
    ppermute x1, waiting for transfers between devices: 0.01 us -> 6.18 us  [body(): lower = lax.ppermute(message, 'space', up)]
    pallas_call x1, Pallas kernels: 11.2 us -> 5.44 us  [forces(): pl.pallas_call(force_kernel, out_shape=jax.ShapeDtypeStruct((groups, 2, 3...]
    pallas_call x2, Pallas kernels: 7.49 us -> 5.09 us  [the longest x1 4.13 us: own_slab(): pl.pallas_call(own_kernel, out_shape=(pltpu.VMEM((beads, atoms // ROWS, 2...]
    unnamed x6 -> x0, local copies, waits for them, and re-layouts: 1.32 us -> none
  transfers between devices with their start and end apart: 3 -> 3, of which waited for: 1 -> 2; matrix products, arithmetic and copies ran while one was open for 0% -> 0% of each run, Pallas kernels for 12% -> 9%
where the time goes in v2:
time: 45.1 us; the launch traced here: 44.8 us
  starting transfers between devices  20.8 us (46%)
  Pallas kernels  12.2 us (27%)
  waiting for transfers between devices  11.2 us (25%)
  between operations  0.67 us (1%)
    ppermute x1, starting transfers between devices, body(): upper = lax.ppermute(message, 'space', down)  13.3 us
    ppermute x1, waiting for transfers between devices, body(): lower = lax.ppermute(message, 'space', up)  6.18 us
    all_to_all x1, starting transfers between devices, body(): everyone = lax.all_to_all(sent, 'bead', 0, 0, tiled=True)  5.55 us
    pallas_call x1, Pallas kernels, forces(): pl.pallas_call(force_kernel, out_shape=jax.ShapeDtypeStruct((groups, 2, 3...  5.44 us
    all_to_all x1, waiting for transfers between devices, body(): everyone = lax.all_to_all(sent, 'bead', 0, 0, tiled=True)  4.98 us
    pallas_call x1, Pallas kernels, own_slab(): pl.pallas_call(own_kernel, out_shape=(pltpu.VMEM((beads, atoms // ROWS, 2...  4.13 us
    ppermute x1, starting transfers between devices, body(): lower = lax.ppermute(message, 'space', up)  1.92 us
    pallas_call x1, Pallas kernels, move_beads(): pl.pallas_call(bead_kernel, out_shape=(jax.ShapeDtypeStruct((3, local, at...  1.67 us
  transfers between devices with their start and end apart: 3, of which 2 were waited for; matrix products, arithmetic and copies ran while one was open for 0% of the time, Pallas kernels for 9%

profile of v2, /device:TPU:2, one launch (start us, length us, event | category | flops | bytes accessed | tf_op | source)
XLA Modules:
  0.0 44.8 jit_solution(10999901525967724912)
XLA Ops:
  0.6 1.0 %pack.1 = bf16[4,144,128]{2,1,0:T(8,128)(2,1)S(1)} custom-call(bf16[4,128,128]{2,1,0:T(8,128)(2,1)} %features.3, f32[3,4,128]{2,1,0:T(4,128)} %bitcast.7, s32[2,1,128]{2,1,0:T(1,128)} %face_map.1), custom_call_target="tpu_custom_call" | custom-call | tf_op jit(solution)/shard_map/pack/pallas_call | solution.py:301
  1.6 13.3 %collective-permute-start.1 = (bf16[4,144,128]{2,1,0:T(8,128)(2,1)S(1)}, bf16[4,144,128]{2,1,0:T(8,128)(2,1)S(1)}, u32[]{:S(2)}, u32[]{:S(2)}) collective-permute-start(bf16[4,144,128]{2,1,0:T(8,128)(2,1)S(1)} %pack.1), channel_id=1, source_target_pairs={{8,0},{16,8},{24,16},{32,24},{40,32},{48,40},{56,48},{64,56},{72,6... | collective-permute-start | bytes 442376 | tf_op jit(solution)/shard_map/ppermute | solution.py:376
  14.9 1.9 %collective-permute-start = (bf16[4,144,128]{2,1,0:T(8,128)(2,1)S(1)}, bf16[4,144,128]{2,1,0:T(8,128)(2,1)S(1)}, u32[]{:S(2)}, u32[]{:S(2)}) collective-permute-start(bf16[4,144,128]{2,1,0:T(8,128)(2,1)S(1)} %pack.1), channel_id=1, source_target_pairs={{0,8},{8,16},{16,24},{24,32},{32,40},{40,48},{48,56},{56,64},{64,7... | collective-permute-start | bytes 442376 | tf_op jit(solution)/shard_map/ppermute | solution.py:377
  16.8 4.1 %own_slab.1 = (bf16[4,8,256,128]{3,2,1,0:T(8,128)(2,1)S(1)}, f32[4,8,128,128]{3,2,1,0:T(8,128)S(1)}, f32[4,3,128,128]{3,2,1,0:T(8,128)S(1)}, s32[128,128]{1,0:T(8,128)S(1)}) custom-call(bf16[4,128,128]{2,1,0:T(8,128)(2,1)} %features.3, s32[64,128]{1,0:T(8,128)} %neighbours.1, s32[64,128]{1,0:T(8,128)} %images.1, f32[3,4,128]{2,1,0:T(4,128)} %bitcast.8, ...), custom_call_target="tpu_custom_call" | custom-call | tf_op jit(solution)/shard_map/own_slab/pallas_call | solution.py:313
  21.0 0.0 collective-permute-done.1.upper
  21.0 6.2 %collective-permute-done.lower = bf16[4,144,128]{2,1,0:T(8,128)(2,1)S(1)} collective-permute-done((bf16[4,144,128]{2,1,0:T(8,128)(2,1)S(1)}, bf16[4,144,128]{2,1,0:T(8,128)(2,1)S(1)}, u32[]{:S(2)}, u32[]{:S(2)}) %collective-permute-start) | collective-permute-done | bytes 147488 | tf_op jit(solution)/shard_map/ppermute | solution.py:377
  27.1 5.4 %forces.1 = f32[8,2,3,4,128]{4,3,2,1,0:T(4,128)} custom-call(bf16[4,144,128]{2,1,0:T(8,128)(2,1)S(1)} %collective-permute-done.lower, bf16[4,144,128]{2,1,0:T(8,128)(2,1)S(1)} %collective-permute-done.1.upper, bf16[4,8,256,128]{3,2,1,0:T(8,128)(2,1)S(1)} %get-tuple-element.8.probes, f32[4,8,128,128]{3,2,1,0:T(8,128)S(1)} %get-tuple-element.9.values, ...), custom_call_target="tpu_custom_call" | custom-call | tf_op jit(solution)/shard_map/forces/pallas_call | solution.py:331
  32.6 5.6 %all-to-all-start = ((f32[8,2,3,4,128]{4,3,2,1,0:T(4,128)}), f32[8,2,3,4,128]{4,3,2,1,0:T(4,128)S(1)}, u32[]{:S(2)}, u32[]{:S(2)}) async-start(f32[8,2,3,4,128]{4,3,2,1,0:T(4,128)} %forces.1), calls=%async_computation | async-start | bytes 196608 | tf_op jit(solution)/shard_map/all_to_all | solution.py:382
  38.1 5.0 %all-to-all-done.everyone = f32[8,2,3,4,128]{4,3,2,1,0:T(4,128)S(1)} async-done(((f32[8,2,3,4,128]{4,3,2,1,0:T(4,128)}), f32[8,2,3,4,128]{4,3,2,1,0:T(4,128)S(1)}, u32[]{:S(2)}, u32[]{:S(2)}) %all-to-all-start) | async-done | bytes 98336 | tf_op jit(solution)/shard_map/all_to_all | solution.py:382
  43.1 1.7 %bead_maps.1 = (f32[3,4,128]{2,1,0:T(4,128)}, f32[3,4,128]{2,1,0:T(4,128)}) custom-call(s32[1]{0:T(128)} %bitcast.group, f32[8,2,3,4,128]{4,3,2,1,0:T(4,128)S(1)} %all-to-all-done.everyone, f32[1,128]{1,0:T(1,128)} %bitcast.12, f32[8,2,8,32]{3,2,1,0:T(8,128)} %constant.6.clone.table), custom_call_target="tpu_custom_call" | custom-call | tf_op jit(solution)/shard_map/bead_maps/pallas_call | solution.py:351
Async XLA Ops:
  1.6 19.4 %collective-permute-start.1 = (bf16[4,144,128]{2,1,0:T(8,128)(2,1)S(1)}, bf16[4,144,128]{2,1,0:T(8,128)(2,1)S(1)}, u32[]{:S(2)}, u32[]{:S(2)}) collective-permute-start(bf16[4,144,128]{2,1,0:T(8,128)(2,1)S(1)} %pack.1), channel_id=1, source_target_pairs={{8,0},{16,8},{24,16},{32,24},{40,32},{48,40},{56,48},{64,56},{72,6... | collective-permute-start | bytes 442376 | tf_op jit(solution)/shard_map/ppermute | solution.py:376
  14.9 12.3 %collective-permute-start = (bf16[4,144,128]{2,1,0:T(8,128)(2,1)S(1)}, bf16[4,144,128]{2,1,0:T(8,128)(2,1)S(1)}, u32[]{:S(2)}, u32[]{:S(2)}) collective-permute-start(bf16[4,144,128]{2,1,0:T(8,128)(2,1)S(1)} %pack.1), channel_id=1, source_target_pairs={{0,8},{8,16},{16,24},{24,32},{32,40},{40,48},{48,56},{56,64},{64,7... | collective-permute-start | bytes 442376 | tf_op jit(solution)/shard_map/ppermute | solution.py:377
  32.6 10.5 %all-to-all-start = ((f32[8,2,3,4,128]{4,3,2,1,0:T(4,128)}), f32[8,2,3,4,128]{4,3,2,1,0:T(4,128)S(1)}, u32[]{:S(2)}, u32[]{:S(2)}) async-start(f32[8,2,3,4,128]{4,3,2,1,0:T(4,128)} %forces.1), calls=%async_computation | async-start | bytes 196608 | tf_op jit(solution)/shard_map/all_to_all | solution.py:382
